TPU v7x, 32 devices: a whole 2x2x4 slice. The times are simulated.
32 devices in a mesh: sec: 2 (over y), gy: 4 (over z), gx: 4 (over x, core).
Axes of the slice: x: 2, y: 2, z: 4, core: 2. Of those that a mesh axis runs over, the one named last changes fastest.
Arguments:
- ocean: bfloat16 [32, 3, 1024, 1536], P(('sec', 'gy'), None, None, 'gx'), may hold values from -6 to 6
- level_weight: float32 [32], replicated, may hold values from 0.25 to 2.5
- velocity_start: float32 [2, 1024, 1536], P(None, ('sec', 'gy'), 'gx'), may hold values from -3 to 3
- wind_stress: float32 [2, 1024, 1536], P(None, ('sec', 'gy'), 'gx'), may hold values from -3 to 3
- thickness: float32 [1024, 1536], P(('sec', 'gy'), 'gx'), may hold values from 0.5 to 2.5
- concentration: float32 [1024, 1536], P(('sec', 'gy'), 'gx'), may hold values from 0.3 to 1
- ice_mask: int32 [1024, 1536], P(('sec', 'gy'), 'gx'), may hold values 0 or 1
- land_mask: int32 [1024, 1536], P(('sec', 'gy'), 'gx'), may hold values 0 or 1
Outputs:
- ice_velocity: float32 [2, 1024, 1536], P(None, ('sec', 'gy'), 'gx')
- ice_stress: float32 [3, 1024, 1536], P(None, ('sec', 'gy'), 'gx')
All inputs are finite; a program needn't handle non-finite values. No bound on the sum of `ice_mask` or of `land_mask` on one device may be relied on, other than what follows from the above.
Results may differ from a plain program's by a relative error of at most 0.0003.
Values may be sent and summed in bfloat16 or wider, within the bound.
A program may use at most 128 MiB of HBM per device.

v0:
```python
import math

import jax
import jax.numpy as jnp
from jax import lax
from jax.sharding import PartitionSpec as P

SUB = 4


ecc_square = 4.0
strain_floor = 0.01
relax_rate = 0.5
water_drag = 0.8
coriolis_f = 0.5
slope_gain = 0.5
conc_decay = 4.0


def extended(block, sides, width):
    for axis, dim in sides:
        count = lax.axis_size(axis)
        forward = [(i, i + 1) for i in range(count - 1)]
        forward.append((count - 1, 0))
        backward = [(target, source) for source, target in forward]
        low = lax.ppermute(
            lax.slice_in_dim(block, block.shape[dim] - width, None, axis=dim), axis, forward
        )
        high = lax.ppermute(lax.slice_in_dim(block, 0, width, axis=dim), axis, backward)
        block = jnp.concatenate([low, block, high], axis=dim)
    return block


def from_behind(value, axis, steps):
    count = lax.axis_size(axis)
    leading, last = (max(0, -steps), min(count, count - steps))
    return lax.ppermute(value, axis, [(source, source + steps) for source in range(leading, last)])


def centre_x(field):
    return 0.5 * (field[..., 1:-1, 2:] - field[..., 1:-1, :-2])


def centre_y(field):
    return 0.5 * (field[..., 2:, 1:-1] - field[..., :-2, 1:-1])


def stresses(velocity, stress, strength, covered):
    east_u = centre_x(velocity[0])
    north_v = centre_y(velocity[1])
    north_u = centre_y(velocity[0])
    east_v = centre_x(velocity[1])
    spread = east_u + north_v
    tension = east_u - north_v
    shear = north_u + east_v
    delta = jnp.sqrt(
        spread * spread + (tension * tension + shear * shear) / ecc_square + strain_floor
    )
    first = (stress[0] + relax_rate * (strength * spread / delta - strength)) / (1.0 + relax_rate)
    second = (stress[1] + relax_rate * strength * tension / (ecc_square * delta)) / (
        1.0 + relax_rate
    )
    third = (stress[2] + relax_rate * strength * shear / (2.0 * ecc_square * delta)) / (
        1.0 + relax_rate
    )
    return jnp.stack([first, second, third]) * covered


def slope_force(height):
    return -slope_gain * jnp.stack([centre_x(height), centre_y(height)])


def momentum(velocity, stress, ice_mass, current, slope, wind_drag, moving):
    normal_x = 0.5 * (stress[0] + stress[1])
    normal_y = 0.5 * (stress[0] - stress[1])
    force_x = centre_x(normal_x) + centre_y(stress[2])
    force_y = centre_x(stress[2]) + centre_y(normal_y)
    rel_u = current[0] - velocity[0]
    rel_v = current[1] - velocity[1]
    drag = water_drag * jnp.sqrt(rel_u * rel_u + rel_v * rel_v)
    diagonal = ice_mass + drag
    turning = coriolis_f * ice_mass
    right_x = (
        ice_mass * velocity[0] + force_x + drag * current[0] + wind_drag[0] + ice_mass * slope[0]
    )
    right_y = (
        ice_mass * velocity[1] + force_y + drag * current[1] + wind_drag[1] + ice_mass * slope[1]
    )
    live = moving > 0.5
    denom = jnp.where(live, diagonal * diagonal + turning * turning, 1.0)
    new_u = jnp.where(live, (diagonal * right_x + turning * right_y) / denom, 0.0)
    new_v = jnp.where(live, (diagonal * right_y - turning * right_x) / denom, 0.0)
    return jnp.stack([new_u, new_v])


def extend(field, width):
    wide = extended(field, (("gx", 2),), width)
    lower = from_behind(wide[:, -width:, :], ("sec", "gy"), 1)
    upper = from_behind(wide[:, :width, :], ("sec", "gy"), -1)
    return jnp.concatenate([lower, wide, upper], axis=1)


def body(
    ocean, level_weight, velocity_start, wind_stress, thickness, concentration, ice_mask, land_mask
):
    level_count = level_weight.shape[0]
    tile_rows = thickness.shape[0]
    tile_cols = thickness.shape[1]
    held = ocean.shape[0]
    own_weights = lax.dynamic_slice_in_dim(level_weight, lax.axis_index(("sec", "gy")) * held, held)

    def add_held(level, total):
        return total + own_weights[level] * ocean[level].astype(jnp.float32)

    summed = lax.fori_loop(
        0,
        held,
        add_held,
        jnp.zeros((3, tile_rows * lax.axis_size(("sec", "gy")), tile_cols), jnp.float32),
    )
    gathered = lax.psum_scatter(
        jnp.transpose(summed, (1, 0, 2)).reshape(
            tile_rows * lax.axis_size(("sec", "gy")), 3 * tile_cols
        ),
        ("sec", "gy"),
        scatter_dimension=0,
        tiled=True,
    )
    surface = jnp.transpose(gathered.reshape(tile_rows, 3, tile_cols), (1, 0, 2)) / math.sqrt(
        level_count
    )
    strength = jnp.exp(-conc_decay * (1.0 - concentration)) * thickness
    covered = ice_mask.astype(jnp.float32)
    moving = covered * land_mask.astype(jnp.float32)
    slope = slope_force(extend(surface[2:3], 1)[0])
    velocity = velocity_start
    stress = jnp.zeros((3, tile_rows, tile_cols), jnp.float32)
    for cycle in range(SUB):
        stress = stresses(extend(velocity, 1), stress, strength, covered)
        velocity = momentum(
            velocity, extend(stress, 1), thickness, surface[0:2], slope, wind_stress, moving
        )
    return (velocity, stress)


def solution(mesh):
    placed = (
        P(("sec", "gy"), None, None, "gx"),
        P(),
        P(None, ("sec", "gy"), "gx"),
        P(None, ("sec", "gy"), "gx"),
        P(("sec", "gy"), "gx"),
        P(("sec", "gy"), "gx"),
        P(("sec", "gy"), "gx"),
        P(("sec", "gy"), "gx"),
    )
    return jax.shard_map(
        body,
        mesh=mesh,
        in_specs=placed,
        out_specs=(P(None, ("sec", "gy"), "gx"), P(None, ("sec", "gy"), "gx")),
        check_vma=False,
    )
```

profile of v0, /device:TPU:25, one launch (start us, length us, event | category | flops | bytes accessed | tf_op | source)
XLA Modules:
  0.0 322.8 jit_solution(1953388586550041366)
XLA Ops:
  8.0 27.2 %while.14 = (s32[]{:T(128)}, f32[3,1024,384]{2,1,0:T(8,128)}, f32[4]{0:T(128)S(1)}, bf16[4,3,1024,384]{3,2,1,0:T(8,128)(2,1)}, s32[]{:T(128)}, /*index=5*/s32[]{:T(128)}) while((s32[]{:T(128)}, f32[3,1024,384]{2,1,0:T(8,128)}, f32[4]{0:T(128)S(1)}, bf16[4,3,1024,384]{3,2,1,0:T(8,128)(2,1)}, s32[]{:T(128)}, ...), condition=%wide.region_1.0_spmd.clone, body=%wide.region_0.0_spmd.clone.sunk | while | flops 4718595 | bytes 11796579 | solution.py:115
  8.5 5.1 %bitcast_add_fusion.2 = f32[3,1024,384]{2,1,0:T(8,128)} fusion(f32[3,1024,384]{2,1,0:T(8,128)} %get-tuple-element.237, bf16[4,3,1024,384]{3,2,1,0:T(8,128)(2,1)} %get-tuple-element.245, s32[]{:T(128)} %get-tuple-element.236, f32[]{:T(128)} %bitcast.260, pred[]{:T(512)S(6)} %compare.3), kind=kLoop, calls=%fused_computation.clone.1 | loop fusion | flops 4718592 | bytes 11796489 | tf_op jit(solution)/shard_map/while/body/eval_jaxpr/add | solution.py:113
  14.3 6.6 %bitcast_add_fusion.2 = f32[3,1024,384]{2,1,0:T(8,128)} fusion(f32[3,1024,384]{2,1,0:T(8,128)} %get-tuple-element.237, bf16[4,3,1024,384]{3,2,1,0:T(8,128)(2,1)} %get-tuple-element.245, s32[]{:T(128)} %get-tuple-element.236, f32[]{:T(128)} %bitcast.260, pred[]{:T(512)S(6)} %compare.3), kind=kLoop, calls=%fused_computation.clone.1 | loop fusion | flops 4718592 | bytes 11796489 | tf_op jit(solution)/shard_map/while/body/eval_jaxpr/add | solution.py:113
  21.4 6.6 %bitcast_add_fusion.2 = f32[3,1024,384]{2,1,0:T(8,128)} fusion(f32[3,1024,384]{2,1,0:T(8,128)} %get-tuple-element.237, bf16[4,3,1024,384]{3,2,1,0:T(8,128)(2,1)} %get-tuple-element.245, s32[]{:T(128)} %get-tuple-element.236, f32[]{:T(128)} %bitcast.260, pred[]{:T(512)S(6)} %compare.3), kind=kLoop, calls=%fused_computation.clone.1 | loop fusion | flops 4718592 | bytes 11796489 | tf_op jit(solution)/shard_map/while/body/eval_jaxpr/add | solution.py:113
  28.6 6.6 %bitcast_add_fusion.2 = f32[3,1024,384]{2,1,0:T(8,128)} fusion(f32[3,1024,384]{2,1,0:T(8,128)} %get-tuple-element.237, bf16[4,3,1024,384]{3,2,1,0:T(8,128)(2,1)} %get-tuple-element.245, s32[]{:T(128)} %get-tuple-element.236, f32[]{:T(128)} %bitcast.260, pred[]{:T(512)S(6)} %compare.3), kind=kLoop, calls=%fused_computation.clone.1 | loop fusion | flops 4718592 | bytes 11796489 | tf_op jit(solution)/shard_map/while/body/eval_jaxpr/add | solution.py:113
  35.2 6.1 %copy.41 = f32[3,1024,384]{1,2,0:T(8,128)} copy(f32[3,1024,384]{2,1,0:T(8,128)} %get-tuple-element.81) | data formatting | bytes 9437184 | tf_op jit(solution)/shard_map/while | solution.py:115
  45.0 2.3 collective-permute-done.1
  47.5 2.8 collective-permute-start.2
  50.3 2.5 collective-permute-start.3
  53.3 22.5 %collective-permute-done.2 = f32[2,1,386]{1,2,0:T(8,128)S(1)} collective-permute-done((f32[2,1,386]{1,2,0:T(8,128)S(1)}, f32[2,1,386]{1,2,0:T(8,128)S(1)}, u32[]{:S(2)}, u32[]{:S(2)}) %collective-permute-start.2) | collective-permute-done | bytes 3120 | tf_op jit(solution)/shard_map/ppermute | solution.py:37
  75.8 10.8 %collective-permute-done.3 = f32[2,1,386]{1,2,0:T(8,128)S(1)} collective-permute-done((f32[2,1,386]{1,2,0:T(8,128)S(1)}, f32[2,1,386]{1,2,0:T(8,128)S(1)}, u32[]{:S(2)}, u32[]{:S(2)}) %collective-permute-start.3) | collective-permute-done | bytes 3120 | tf_op jit(solution)/shard_map/ppermute | solution.py:37
  89.9 2.7 collective-permute-done.5
  99.1 3.4 %collective-permute-start.7 = (f32[3,1,386]{2,1,0:T(1,128)}, f32[3,1,386]{2,1,0:T(1,128)}, u32[]{:S(2)}, u32[]{:S(2)}) collective-permute-start(f32[3,1,386]{2,1,0:T(1,128)} %copy.52), channel_id=1, source_target_pairs={{4,0},{8,4},{12,8},{16,12},{20,16},{24,20},{28,24},{5,1},{9,5},{13... | collective-permute-start | bytes 13904 | tf_op jit(solution)/shard_map/ppermute | solution.py:37
  108.5 46.1 %reduce-scatter.2.cloned.1.call-done = f32[128,1152]{0,1:T(8,128)} async-done(((f32[1024,1152]{0,1:T(8,128)}), f32[128,1152]{0,1:T(8,128)}) %reduce-scatter.2.cloned.1.call-update) | async-done | bytes 589840 | tf_op jit(solution)/shard_map/reduce_scatter | solution.py:121
  160.7 4.3 %collective-permute-start.10 = (f32[1,1,386]{1,2,0:T(8,128)S(1)}, f32[1,1,386]{1,2,0:T(8,128)S(1)}, u32[]{:S(2)}, u32[]{:S(2)}) collective-permute-start(f32[1,1,386]{1,2,0:T(8,128)S(1)} %get-tuple-element.203), channel_id=1, source_target_pairs={{0,4},{4,8},{8,12},{12,16},{16,20},{20,24},{24,28},{1,5},{5,9},{9,... | collective-permute-start | bytes 4640 | tf_op jit(solution)/shard_map/ppermute | solution.py:37
  167.0 2.8 collective-permute-done.10
  169.8 6.2 %collective-permute-done.11 = f32[1,1,386]{1,2,0:T(8,128)S(1)} collective-permute-done((f32[1,1,386]{1,2,0:T(8,128)S(1)}, f32[1,1,386]{1,2,0:T(8,128)S(1)}, u32[]{:S(2)}, u32[]{:S(2)}) %collective-permute-start.11) | collective-permute-done | bytes 1576 | tf_op jit(solution)/shard_map/ppermute | solution.py:37
  184.2 3.4 %collective-permute-start.15 = (f32[2,1,386]{1,2,0:T(8,128)S(1)}, f32[2,1,386]{1,2,0:T(8,128)S(1)}, u32[]{:S(2)}, u32[]{:S(2)}) collective-permute-start(f32[2,1,386]{1,2,0:T(8,128)S(1)} %get-tuple-element.188), channel_id=1, source_target_pairs={{4,0},{8,4},{12,8},{16,12},{20,16},{24,20},{28,24},{5,1},{9,5},{13... | collective-permute-start | bytes 9272 | tf_op jit(solution)/shard_map/ppermute | solution.py:37
  187.5 7.6 %collective-permute-done.14 = f32[2,1,386]{1,2,0:T(8,128)S(1)} collective-permute-done((f32[2,1,386]{1,2,0:T(8,128)S(1)}, f32[2,1,386]{1,2,0:T(8,128)S(1)}, u32[]{:S(2)}, u32[]{:S(2)}) %collective-permute-start.14) | collective-permute-done | bytes 3120 | tf_op jit(solution)/shard_map/ppermute | solution.py:37
  195.2 6.3 %collective-permute-done.15 = f32[2,1,386]{1,2,0:T(8,128)S(1)} collective-permute-done((f32[2,1,386]{1,2,0:T(8,128)S(1)}, f32[2,1,386]{1,2,0:T(8,128)S(1)}, u32[]{:S(2)}, u32[]{:S(2)}) %collective-permute-start.15) | collective-permute-done | bytes 3120 | tf_op jit(solution)/shard_map/ppermute | solution.py:37
  205.0 2.3 collective-permute-done.17
  213.1 3.5 %collective-permute-start.19 = (f32[3,1,386]{2,1,0:T(1,128)S(1)}, f32[3,1,386]{2,1,0:T(1,128)S(1)}, u32[]{:S(2)}, u32[]{:S(2)}) collective-permute-start(f32[3,1,386]{2,1,0:T(1,128)S(1)} %copy.64), channel_id=1, source_target_pairs={{4,0},{8,4},{12,8},{16,12},{20,16},{24,20},{28,24},{5,1},{9,5},{13... | collective-permute-start | bytes 13904 | tf_op jit(solution)/shard_map/ppermute | solution.py:37
  217.7 2.4 collective-permute-done.19
  230.2 3.5 %collective-permute-start.23 = (f32[2,1,386]{1,2,0:T(8,128)S(1)}, f32[2,1,386]{1,2,0:T(8,128)S(1)}, u32[]{:S(2)}, u32[]{:S(2)}) collective-permute-start(f32[2,1,386]{1,2,0:T(8,128)S(1)} %get-tuple-element.186), channel_id=1, source_target_pairs={{4,0},{8,4},{12,8},{16,12},{20,16},{24,20},{28,24},{5,1},{9,5},{13... | collective-permute-start | bytes 9272 | tf_op jit(solution)/shard_map/ppermute | solution.py:37
  233.8 7.3 %collective-permute-done.22 = f32[2,1,386]{1,2,0:T(8,128)S(1)} collective-permute-done((f32[2,1,386]{1,2,0:T(8,128)S(1)}, f32[2,1,386]{1,2,0:T(8,128)S(1)}, u32[]{:S(2)}, u32[]{:S(2)}) %collective-permute-start.22) | collective-permute-done | bytes 3120 | tf_op jit(solution)/shard_map/ppermute | solution.py:37
  241.0 6.2 %collective-permute-done.23 = f32[2,1,386]{1,2,0:T(8,128)S(1)} collective-permute-done((f32[2,1,386]{1,2,0:T(8,128)S(1)}, f32[2,1,386]{1,2,0:T(8,128)S(1)}, u32[]{:S(2)}, u32[]{:S(2)}) %collective-permute-start.23) | collective-permute-done | bytes 3120 | tf_op jit(solution)/shard_map/ppermute | solution.py:37
  250.8 2.3 collective-permute-done.25
  259.0 3.9 %collective-permute-start.27 = (f32[3,1,386]{2,1,0:T(1,128)S(1)}, f32[3,1,386]{2,1,0:T(1,128)S(1)}, u32[]{:S(2)}, u32[]{:S(2)}) collective-permute-start(f32[3,1,386]{2,1,0:T(1,128)S(1)} %copy.71), channel_id=1, source_target_pairs={{4,0},{8,4},{12,8},{16,12},{20,16},{24,20},{28,24},{5,1},{9,5},{13... | collective-permute-start | bytes 13904 | tf_op jit(solution)/shard_map/ppermute | solution.py:37
  276.2 3.4 %collective-permute-start.31 = (f32[2,1,386]{1,2,0:T(8,128)S(1)}, f32[2,1,386]{1,2,0:T(8,128)S(1)}, u32[]{:S(2)}, u32[]{:S(2)}) collective-permute-start(f32[2,1,386]{1,2,0:T(8,128)S(1)} %get-tuple-element.184), channel_id=1, source_target_pairs={{4,0},{8,4},{12,8},{16,12},{20,16},{24,20},{28,24},{5,1},{9,5},{13... | collective-permute-start | bytes 9272 | tf_op jit(solution)/shard_map/ppermute | solution.py:37
  279.6 6.7 %collective-permute-done.30 = f32[2,1,386]{1,2,0:T(8,128)S(1)} collective-permute-done((f32[2,1,386]{1,2,0:T(8,128)S(1)}, f32[2,1,386]{1,2,0:T(8,128)S(1)}, u32[]{:S(2)}, u32[]{:S(2)}) %collective-permute-start.30) | collective-permute-done | bytes 3120 | tf_op jit(solution)/shard_map/ppermute | solution.py:37
  286.3 6.2 %collective-permute-done.31 = f32[2,1,386]{1,2,0:T(8,128)S(1)} collective-permute-done((f32[2,1,386]{1,2,0:T(8,128)S(1)}, f32[2,1,386]{1,2,0:T(8,128)S(1)}, u32[]{:S(2)}, u32[]{:S(2)}) %collective-permute-start.31) | collective-permute-done | bytes 3120 | tf_op jit(solution)/shard_map/ppermute | solution.py:37
  304.3 4.0 %collective-permute-start.35 = (f32[3,1,386]{2,1,0:T(1,128)S(1)}, f32[3,1,386]{2,1,0:T(1,128)S(1)}, u32[]{:S(2)}, u32[]{:S(2)}) collective-permute-start(f32[3,1,386]{2,1,0:T(1,128)S(1)} %copy.78), channel_id=1, source_target_pairs={{4,0},{8,4},{12,8},{16,12},{20,16},{24,20},{28,24},{5,1},{9,5},{13... | collective-permute-start | bytes 13904 | tf_op jit(solution)/shard_map/ppermute | solution.py:37
  (171 shorter events, 101.9 us)
Async XLA Ops:
  7.2 147.4 %reduce-scatter.2.cloned.1.call-start = ((), (), s32[]{:S(2)}) async-start(), calls=%async_computation.1 | async-start | bytes 5308416 | tf_op jit(solution)/shard_map/reduce_scatter | solution.py:121
  42.5 2.6 collective-permute-start
  44.3 3.0 collective-permute-start.1
  47.5 28.3 %collective-permute-start.2 = (f32[2,1,386]{1,2,0:T(8,128)S(1)}, f32[2,1,386]{1,2,0:T(8,128)S(1)}, u32[]{:S(2)}, u32[]{:S(2)}) collective-permute-start(f32[2,1,386]{1,2,0:T(8,128)S(1)} %get-tuple-element.191), channel_id=1, source_target_pairs={{0,4},{4,8},{8,12},{12,16},{16,20},{20,24},{24,28},{1,5},{5,9},{9,... | collective-permute-start | bytes 9272 | tf_op jit(solution)/shard_map/ppermute | solution.py:37
  50.3 36.3 %collective-permute-start.3 = (f32[2,1,386]{1,2,0:T(8,128)S(1)}, f32[2,1,386]{1,2,0:T(8,128)S(1)}, u32[]{:S(2)}, u32[]{:S(2)}) collective-permute-start(f32[2,1,386]{1,2,0:T(8,128)S(1)} %get-tuple-element.192), channel_id=1, source_target_pairs={{4,0},{8,4},{12,8},{16,12},{20,16},{24,20},{28,24},{5,1},{9,5},{13... | collective-permute-start | bytes 9272 | tf_op jit(solution)/shard_map/ppermute | solution.py:37
  89.1 3.4 %collective-permute-start.5 = (f32[3,128,1]{1,2,0:T(1,128)S(1)}, f32[3,128,1]{1,2,0:T(1,128)S(1)}, u32[]{:S(2)}, u32[]{:S(2)}) collective-permute-start(f32[3,128,1]{1,2,0:T(1,128)S(1)} %get-tuple-element.182), channel_id=1, source_target_pairs={{1,0},{2,1},{3,2},{0,3},{5,4},{6,5},{7,6},{4,7},{9,8},{10,9},{11,1... | collective-permute-start | bytes 4616 | tf_op jit(solution)/shard_map/ppermute | solution.py:29
  96.2 7.4 %collective-permute-start.6 = (f32[3,1,386]{2,1,0:T(1,128)}, f32[3,1,386]{2,1,0:T(1,128)}, u32[]{:S(2)}, u32[]{:S(2)}) collective-permute-start(f32[3,1,386]{2,1,0:T(1,128)} %copy.51), channel_id=1, source_target_pairs={{0,4},{4,8},{8,12},{12,16},{16,20},{20,24},{24,28},{1,5},{5,9},{9,... | collective-permute-start | bytes 13904 | tf_op jit(solution)/shard_map/ppermute | solution.py:37
  99.1 7.6 %collective-permute-start.7 = (f32[3,1,386]{2,1,0:T(1,128)}, f32[3,1,386]{2,1,0:T(1,128)}, u32[]{:S(2)}, u32[]{:S(2)}) collective-permute-start(f32[3,1,386]{2,1,0:T(1,128)} %copy.52), channel_id=1, source_target_pairs={{4,0},{8,4},{12,8},{16,12},{20,16},{24,20},{28,24},{5,1},{9,5},{13... | collective-permute-start | bytes 13904 | tf_op jit(solution)/shard_map/ppermute | solution.py:37
  155.7 2.5 collective-permute-start.8
  157.5 3.0 collective-permute-start.9
  160.7 9.2 %collective-permute-start.10 = (f32[1,1,386]{1,2,0:T(8,128)S(1)}, f32[1,1,386]{1,2,0:T(8,128)S(1)}, u32[]{:S(2)}, u32[]{:S(2)}) collective-permute-start(f32[1,1,386]{1,2,0:T(8,128)S(1)} %get-tuple-element.203), channel_id=1, source_target_pairs={{0,4},{4,8},{8,12},{12,16},{16,20},{20,24},{24,28},{1,5},{5,9},{9,... | collective-permute-start | bytes 4640 | tf_op jit(solution)/shard_map/ppermute | solution.py:37
  165.0 11.0 %collective-permute-start.11 = (f32[1,1,386]{1,2,0:T(8,128)S(1)}, f32[1,1,386]{1,2,0:T(8,128)S(1)}, u32[]{:S(2)}, u32[]{:S(2)}) collective-permute-start(f32[1,1,386]{1,2,0:T(8,128)S(1)} %get-tuple-element.204), channel_id=1, source_target_pairs={{4,0},{8,4},{12,8},{16,12},{20,16},{24,20},{28,24},{5,1},{9,5},{13... | collective-permute-start | bytes 4640 | tf_op jit(solution)/shard_map/ppermute | solution.py:37
  179.0 3.0 collective-permute-start.13
  182.2 12.9 %collective-permute-start.14 = (f32[2,1,386]{1,2,0:T(8,128)S(1)}, f32[2,1,386]{1,2,0:T(8,128)S(1)}, u32[]{:S(2)}, u32[]{:S(2)}) collective-permute-start(f32[2,1,386]{1,2,0:T(8,128)S(1)} %get-tuple-element.187), channel_id=1, source_target_pairs={{0,4},{4,8},{8,12},{12,16},{16,20},{20,24},{24,28},{1,5},{5,9},{9,... | collective-permute-start | bytes 9272 | tf_op jit(solution)/shard_map/ppermute | solution.py:37
  184.2 17.3 %collective-permute-start.15 = (f32[2,1,386]{1,2,0:T(8,128)S(1)}, f32[2,1,386]{1,2,0:T(8,128)S(1)}, u32[]{:S(2)}, u32[]{:S(2)}) collective-permute-start(f32[2,1,386]{1,2,0:T(8,128)S(1)} %get-tuple-element.188), channel_id=1, source_target_pairs={{4,0},{8,4},{12,8},{16,12},{20,16},{24,20},{28,24},{5,1},{9,5},{13... | collective-permute-start | bytes 9272 | tf_op jit(solution)/shard_map/ppermute | solution.py:37
  204.2 3.0 collective-permute-start.17
  209.8 6.8 %collective-permute-start.18 = (f32[3,1,386]{2,1,0:T(1,128)S(1)}, f32[3,1,386]{2,1,0:T(1,128)S(1)}, u32[]{:S(2)}, u32[]{:S(2)}) collective-permute-start(f32[3,1,386]{2,1,0:T(1,128)S(1)} %copy.63), channel_id=1, source_target_pairs={{0,4},{4,8},{8,12},{12,16},{16,20},{20,24},{24,28},{1,5},{5,9},{9,... | collective-permute-start | bytes 13904 | tf_op jit(solution)/shard_map/ppermute | solution.py:37
  213.1 7.1 %collective-permute-start.19 = (f32[3,1,386]{2,1,0:T(1,128)S(1)}, f32[3,1,386]{2,1,0:T(1,128)S(1)}, u32[]{:S(2)}, u32[]{:S(2)}) collective-permute-start(f32[3,1,386]{2,1,0:T(1,128)S(1)} %copy.64), channel_id=1, source_target_pairs={{4,0},{8,4},{12,8},{16,12},{20,16},{24,20},{28,24},{5,1},{9,5},{13... | collective-permute-start | bytes 13904 | tf_op jit(solution)/shard_map/ppermute | solution.py:37
  225.1 3.0 collective-permute-start.21
  228.3 12.7 %collective-permute-start.22 = (f32[2,1,386]{1,2,0:T(8,128)S(1)}, f32[2,1,386]{1,2,0:T(8,128)S(1)}, u32[]{:S(2)}, u32[]{:S(2)}) collective-permute-start(f32[2,1,386]{1,2,0:T(8,128)S(1)} %get-tuple-element.185), channel_id=1, source_target_pairs={{0,4},{4,8},{8,12},{12,16},{16,20},{20,24},{24,28},{1,5},{5,9},{9,... | collective-permute-start | bytes 9272 | tf_op jit(solution)/shard_map/ppermute | solution.py:37
  230.2 17.0 %collective-permute-start.23 = (f32[2,1,386]{1,2,0:T(8,128)S(1)}, f32[2,1,386]{1,2,0:T(8,128)S(1)}, u32[]{:S(2)}, u32[]{:S(2)}) collective-permute-start(f32[2,1,386]{1,2,0:T(8,128)S(1)} %get-tuple-element.186), channel_id=1, source_target_pairs={{4,0},{8,4},{12,8},{16,12},{20,16},{24,20},{28,24},{5,1},{9,5},{13... | collective-permute-start | bytes 9272 | tf_op jit(solution)/shard_map/ppermute | solution.py:37
  248.5 2.3 collective-permute-start.24
  250.1 3.0 collective-permute-start.25
  255.7 7.1 %collective-permute-start.26 = (f32[3,1,386]{2,1,0:T(1,128)S(1)}, f32[3,1,386]{2,1,0:T(1,128)S(1)}, u32[]{:S(2)}, u32[]{:S(2)}) collective-permute-start(f32[3,1,386]{2,1,0:T(1,128)S(1)} %copy.70), channel_id=1, source_target_pairs={{0,4},{4,8},{8,12},{12,16},{16,20},{20,24},{24,28},{1,5},{5,9},{9,... | collective-permute-start | bytes 13904 | tf_op jit(solution)/shard_map/ppermute | solution.py:37
  259.0 7.2 %collective-permute-start.27 = (f32[3,1,386]{2,1,0:T(1,128)S(1)}, f32[3,1,386]{2,1,0:T(1,128)S(1)}, u32[]{:S(2)}, u32[]{:S(2)}) collective-permute-start(f32[3,1,386]{2,1,0:T(1,128)S(1)} %copy.71), channel_id=1, source_target_pairs={{4,0},{8,4},{12,8},{16,12},{20,16},{24,20},{28,24},{5,1},{9,5},{13... | collective-permute-start | bytes 13904 | tf_op jit(solution)/shard_map/ppermute | solution.py:37
  271.0 3.0 collective-permute-start.29
  274.3 12.0 %collective-permute-start.30 = (f32[2,1,386]{1,2,0:T(8,128)S(1)}, f32[2,1,386]{1,2,0:T(8,128)S(1)}, u32[]{:S(2)}, u32[]{:S(2)}) collective-permute-start(f32[2,1,386]{1,2,0:T(8,128)S(1)} %get-tuple-element.183), channel_id=1, source_target_pairs={{0,4},{4,8},{8,12},{12,16},{16,20},{20,24},{24,28},{1,5},{5,9},{9,... | collective-permute-start | bytes 9272 | tf_op jit(solution)/shard_map/ppermute | solution.py:37
  276.2 16.3 %collective-permute-start.31 = (f32[2,1,386]{1,2,0:T(8,128)S(1)}, f32[2,1,386]{1,2,0:T(8,128)S(1)}, u32[]{:S(2)}, u32[]{:S(2)}) collective-permute-start(f32[2,1,386]{1,2,0:T(8,128)S(1)} %get-tuple-element.184), channel_id=1, source_target_pairs={{4,0},{8,4},{12,8},{16,12},{20,16},{24,20},{28,24},{5,1},{9,5},{13... | collective-permute-start | bytes 9272 | tf_op jit(solution)/shard_map/ppermute | solution.py:37
  293.8 2.4 collective-permute-start.32
  295.4 3.0 collective-permute-start.33
  301.0 8.3 %collective-permute-start.34 = (f32[3,1,386]{2,1,0:T(1,128)S(1)}, f32[3,1,386]{2,1,0:T(1,128)S(1)}, u32[]{:S(2)}, u32[]{:S(2)}) collective-permute-start(f32[3,1,386]{2,1,0:T(1,128)S(1)} %copy.77), channel_id=1, source_target_pairs={{0,4},{4,8},{8,12},{12,16},{16,20},{20,24},{24,28},{1,5},{5,9},{9,... | collective-permute-start | bytes 13904 | tf_op jit(solution)/shard_map/ppermute | solution.py:37
  304.3 7.1 %collective-permute-start.35 = (f32[3,1,386]{2,1,0:T(1,128)S(1)}, f32[3,1,386]{2,1,0:T(1,128)S(1)}, u32[]{:S(2)}, u32[]{:S(2)}) collective-permute-start(f32[3,1,386]{2,1,0:T(1,128)S(1)} %copy.78), channel_id=1, source_target_pairs={{4,0},{8,4},{12,8},{16,12},{20,16},{24,20},{28,24},{5,1},{9,5},{13... | collective-permute-start | bytes 13904 | tf_op jit(solution)/shard_map/ppermute | solution.py:37
  (15 other events, 109.1 us)
Sparse Core Ops, SparseCore 0:
  41.4 113.0 reduce-scatter.1
where the time goes:
time: 327 us; the launch traced here: 323 us
  waiting for transfers between devices  163 us (50%)
  starting transfers between devices  63.3 us (19%)
  local copies, waits for them, and re-layouts  40.9 us (13%)
  other arithmetic  40.6 us (12%)
  between operations  14.7 us (4%)
    ppermute x18, waiting for transfers between devices, from_behind(): lax.ppermute(value, axis, [(source, source + steps) for source in range(l...  90.4 us
    ppermute x18, starting transfers between devices, from_behind(): lax.ppermute(value, axis, [(source, source + steps) for source in range(l...  50 us
    reduce_scatter x1, waiting for transfers between devices, body(): lax.psum_scatter(jnp.transpose(summed, (1, 0, 2)).reshape(tile_rows * lax...  46.1 us
    add x4, other arithmetic, add_held(): return total + own_weights[level] * ocean[level].astype(jnp.float32)  24.9 us
    ppermute x9, waiting for transfers between devices, extended(): lax.ppermute(lax.slice_in_dim(block, 0, width, axis=dim), axis, backward)  20.9 us
    ppermute x9, starting transfers between devices, extended(): lax.ppermute(lax.slice_in_dim(block, block.shape[dim] - width, None, axis...  13.2 us
    slice x13, local copies, waits for them, and re-layouts, extend(): lower = from_behind(wide[:, -width:, :], ('sec', 'gy'), 1)  11.5 us
    ppermute x8, local copies, waits for them, and re-layouts, from_behind(): lax.ppermute(value, axis, [(source, source + steps) for source in range(l...  9.32 us
  transfers between devices with their start and end apart: 37, of which 33 were waited for; matrix products, arithmetic and copies ran while one was open for 6% of the time, Pallas kernels for 0%

commit v1 on v0

v1 whole, which is shorter than its diff:
```python
import functools
import math

import jax
import jax.numpy as jnp
from jax import lax
from jax.experimental import pallas as pl
from jax.experimental.pallas import tpu as pltpu
from jax.sharding import PartitionSpec as P

SUB = 4
HALO = 8
LANES = 128
MESH = pl.DeviceIdType.MESH

U, V, WX, WY, THICK, STRENGTH, COVERED, MOVING = range(8)
FIELDS = 8


def kernel(
    dims,
    weight_ref,
    ocean_hbm,
    vel_hbm,
    wind_hbm,
    thick_hbm,
    conc_hbm,
    ice_hbm,
    land_hbm,
    vel_out,
    stress_out,
    ocean,
    total,
    y_send,
    y_recv,
    y_send_scale,
    y_recv_scale,
    z_send,
    z_recv,
    z_send_scale,
    z_recv_scale,
    own,
    masks,
    fields,
    stress,
    surf,
    ns_field,
    ew_field,
    ns_surf,
    ew_surf,
    ocean_sem,
    static_sem,
    y_sems,
    z_sems,
    ns_sems,
    ew_sems,
    out_sem,
):
    secs, rows_g, cols_g, levels = dims
    held = ocean_hbm.shape[0]
    tile_rows, tile_cols = thick_hbm.shape
    tiles = tile_cols // LANES
    top = 2 * HALO
    end = top + tile_rows
    s, g, x = lax.axis_index("sec"), lax.axis_index("gy"), lax.axis_index("gx")
    ranks = secs * rows_g
    rank = s * rows_g + g

    def at_rank(number):
        number = lax.rem(number + ranks, ranks)
        return (number // rows_g, lax.rem(number, rows_g), x)

    north, south = at_rank(rank - 1), at_rank(rank + 1)
    west = (s, g, lax.rem(x + cols_g - 1, cols_g))
    east = (s, g, lax.rem(x + 1, cols_g))
    over_secs = [(lax.rem(s + i, secs), g, x) for i in range(1, secs)]
    over_rows = [(s, lax.rem(g + k, rows_g), x) for k in range(1, rows_g)]

    order = [rows_g // 2] + [k for k in range(1, rows_g) if k != rows_g // 2] + [0]

    def block_rows(sec, k):
        block = sec * rows_g + lax.rem(g + k, rows_g)
        return pl.ds(pl.multiple_of(block * tile_rows, tile_rows), tile_rows)

    ocean_copies = {}
    for i in list(range(1, secs)) + [0]:
        for k in order:
            at = block_rows(lax.rem(s + i, secs), k)
            copy = pltpu.make_async_copy(
                ocean_hbm.at[:, :, at, :], ocean.at[i * rows_g + k], ocean_sem.at[i * rows_g + k]
            )
            copy.start()
            ocean_copies[i, k] = copy
    static_copies = []
    for j in range(tiles):
        cols = pl.ds(j * LANES, LANES)
        rows = pl.ds(top, tile_rows)
        for n, (source, target) in enumerate(
            (
                (vel_hbm.at[:, :, cols], fields.at[pl.ds(U, 2), j, rows, :]),
                (wind_hbm.at[:, :, cols], fields.at[pl.ds(WX, 2), j, rows, :]),
                (thick_hbm.at[:, cols], fields.at[THICK, j, rows, :]),
                (conc_hbm.at[:, cols], fields.at[STRENGTH, j, rows, :]),
                (ice_hbm.at[:, cols], masks.at[0, j]),
                (land_hbm.at[:, cols], masks.at[1, j]),
            )
        ):
            copy = pltpu.make_async_copy(source, target, static_sem.at[j, n])
            copy.start()
            static_copies.append(copy)

    barrier = pltpu.get_barrier_semaphore()
    partners = over_secs + over_rows + [north, south, west, east]
    for partner in partners:
        pl.semaphore_signal(barrier, inc=1, device_id=partner, device_id_type=MESH)
    pl.semaphore_wait(barrier, len(partners))

    def remote(source, target, sems, device):
        return pltpu.make_async_remote_copy(
            src_ref=source,
            dst_ref=target,
            send_sem=sems.at[0],
            recv_sem=sems.at[1],
            device_id=device,
            device_id_type=MESH,
        )

    own_weights = [weight_ref[rank * held + k] for k in range(held)]
    strips = tile_rows // 16

    def level_sum(slot, c, at, j):
        cols = pl.ds(j * LANES, LANES)
        value = own_weights[0] * ocean[slot, 0, c, at, cols].astype(jnp.float32)
        for k in range(1, held):
            value = value + own_weights[k] * ocean[slot, k, c, at, cols].astype(jnp.float32)
        return value

    def twice(value):
        return jnp.concatenate([value, value], axis=0)

    def coded(value_of, target, scale_ref):
        def first(i, most):
            at = pl.ds(pl.multiple_of(i * 16, 16), 16)
            for j in range(tiles):
                value = value_of(at, j)
                total[at, pl.ds(j * LANES, LANES)] = value
                most = jnp.maximum(most, jnp.abs(value))
            return most

        most = lax.fori_loop(0, strips, first, jnp.zeros((16, LANES), jnp.float32))
        most = jnp.maximum(jnp.maximum(most[0:8], most[8:16]), 1e-30)
        scale_ref[...] = most * (1.0 / 32767.0)
        inverse = twice(32767.0 / most)

        @pl.loop(0, strips)
        def _(i):
            at = pl.ds(pl.multiple_of(i * 16, 16), 16)
            for j in range(tiles):
                cols = pl.ds(j * LANES, LANES)
                code = jnp.round(total[at, cols] * inverse)
                target[at, cols] = code.astype(jnp.int32).astype(jnp.int16)

    def decoded(code_ref, scale, at, j):
        code = code_ref[at, pl.ds(j * LANES, LANES)].astype(jnp.int32)
        return code.astype(jnp.float32) * scale

    y_copies = {}
    for i in range(1, secs):
        for k in order:
            ocean_copies[i, k].wait()
            for c in range(3):
                slot = ((i - 1) * rows_g + k, c)
                coded(
                    lambda at, j, i=i, k=k, c=c: level_sum(i * rows_g + k, c, at, j),
                    y_send.at[slot],
                    y_send_scale.at[slot],
                )
                pair = (
                    remote(y_send.at[slot], y_recv.at[slot], y_sems.at[slot + (0,)], over_secs[i - 1]),
                    remote(
                        y_send_scale.at[slot],
                        y_recv_scale.at[slot],
                        y_sems.at[slot + (1,)],
                        over_secs[i - 1],
                    ),
                )
                for copy in pair:
                    copy.start()
                y_copies[i, k, c] = pair

    for copy in static_copies:
        copy.wait()

    @pl.loop(0, tile_rows // 8)
    def _(i):
        at = pl.ds(pl.multiple_of(i * 8, 8), 8)
        to = pl.ds(pl.multiple_of(i * 8 + top, 8), 8)
        for j in range(tiles):
            conc = fields[STRENGTH, j, to, :]
            fields[STRENGTH, j, to, :] = jnp.exp(-4.0 * (1.0 - conc)) * fields[THICK, j, to, :]
            ice = masks[0, j, at, :].astype(jnp.float32)
            fields[COVERED, j, to, :] = ice
            fields[MOVING, j, to, :] = ice * masks[1, j, at, :].astype(jnp.float32)

    inner = pl.ds(0, tiles)

    def send_rows(source, target, sems):
        up = remote(
            source.at[:, inner, pl.ds(top, HALO), :], target.at[1], sems.at[0], north
        )
        down = remote(
            source.at[:, inner, pl.ds(end - HALO, HALO), :], target.at[0], sems.at[1], south
        )
        up.start()
        down.start()
        return up, down

    def place_rows(target, received, count):
        above = jnp.where(rank > 0, 1.0, 0.0)
        below = jnp.where(rank < ranks - 1, 1.0, 0.0)
        for f in range(count):
            for j in range(tiles):
                target[f, j, pl.ds(HALO, HALO), :] = received[0, f, j] * above
                target[f, j, pl.ds(end, HALO), :] = received[1, f, j] * below

    full = pl.ds(HALO, tile_rows + 2 * HALO)

    def send_columns(source, target, sems):
        left = remote(source.at[:, 0, full, :], target.at[1], sems.at[0], west)
        right = remote(source.at[:, tiles - 1, full, :], target.at[0], sems.at[1], east)
        left.start()
        right.start()
        return left, right

    lane = lax.broadcasted_iota(jnp.int32, (8, LANES), 1)
    all_strips = (tile_rows + 2 * HALO) // 8

    def place_columns(target, received, count):
        @pl.loop(0, all_strips)
        def _(i):
            at = pl.ds(pl.multiple_of(i * 8, 8), 8)
            to = pl.ds(pl.multiple_of(i * 8 + HALO, 8), 8)
            for f in range(count):
                target[f, tiles, to, :] = jnp.where(
                    lane < HALO,
                    received[1, f, at, :],
                    jnp.where(lane >= LANES - HALO, received[0, f, at, :], 0.0),
                )

    field_rows = send_rows(fields, ns_field, ns_sems.at[0])

    z_copies = []
    field_columns = None
    for k in order:
        ocean_copies[0, k].wait()
        for c in range(3):
            slots = [((i - 1) * rows_g + k, c) for i in range(1, secs)]
            for i in range(1, secs):
                for copy in y_copies[i, k, c]:
                    copy.wait_recv()
            scales = [twice(y_recv_scale[slot]) for slot in slots]

            def value_of(at, j, k=k, c=c, slots=slots, scales=scales):
                value = level_sum(k, c, at, j)
                for slot, scale in zip(slots, scales):
                    value = value + decoded(y_recv.at[slot], scale, at, j)
                return value

            if k == 0:

                @pl.loop(0, strips)
                def _(i, value_of=value_of, c=c):
                    at = pl.ds(pl.multiple_of(i * 16, 16), 16)
                    for j in range(tiles):
                        own[c, at, pl.ds(j * LANES, LANES)] = value_of(at, j)
            else:
                slot = (k - 1, c)
                coded(value_of, z_send.at[slot], z_send_scale.at[slot])
                pair = (
                    remote(z_send.at[slot], z_recv.at[slot], z_sems.at[slot + (0,)], over_rows[k - 1]),
                    remote(
                        z_send_scale.at[slot],
                        z_recv_scale.at[slot],
                        z_sems.at[slot + (1,)],
                        over_rows[k - 1],
                    ),
                )
                for copy in pair:
                    copy.start()
                z_copies.append(pair)
        if k == order[0]:
            for copy in field_rows:
                copy.wait()
            place_rows(fields, ns_field, FIELDS)
            field_columns = send_columns(fields, ew_field, ew_sems.at[0])

    for copy in field_columns:
        copy.wait()
    place_columns(fields, ew_field, FIELDS)
    every = tiles + 1

    def margins(target, count):
        zero = jnp.zeros((8, LANES), jnp.float32)
        for f in range(count):
            for j in range(every):
                target[f, j, pl.ds(0, HALO), :] = zero
                target[f, j, pl.ds(end + HALO, HALO), :] = zero

    margins(fields, 2)
    margins(stress, 3)
    margins(surf, 3)

    def sides(values):
        before = [pltpu.roll(value, 1, 1) for value in values]
        after = [pltpu.roll(value, LANES - 1, 1) for value in values]
        out = []
        for j in range(every):
            low = jnp.where(lane == 0, before[j - 1], before[j])
            high = jnp.where(lane == LANES - 1, after[(j + 1) % every], after[j])
            out.append(0.5 * (high - low))
        return out

    def strip_rows(i, shift):
        if shift == 0:
            return pl.ds(pl.multiple_of(i * 8 + HALO, 8), 8)
        return pl.ds(i * 8 + HALO + shift, 8)

    def rows_of(ref, f, at):
        return [ref[f, j, at, :] for j in range(every)]

    def stress_step(first):
        @pl.loop(0, all_strips)
        def _(i):
            at, up, down = strip_rows(i, 0), strip_rows(i, -1), strip_rows(i, 1)
            east_u = sides(rows_of(fields, U, at))
            east_v = sides(rows_of(fields, V, at))
            for j in range(every):
                north_u = 0.5 * (fields[U, j, down, :] - fields[U, j, up, :])
                north_v = 0.5 * (fields[V, j, down, :] - fields[V, j, up, :])
                spread = east_u[j] + north_v
                tension = east_u[j] - north_v
                shear = north_u + east_v[j]
                turned = lax.rsqrt(
                    spread * spread + 0.25 * (tension * tension + shear * shear) + 0.01
                )
                half = 0.5 * fields[STRENGTH, j, at, :]
                rate = half * turned
                covered = fields[COVERED, j, at, :] * (1.0 / 1.5)
                new0 = rate * spread - half
                new1 = (0.25 * rate) * tension
                new2 = (0.125 * rate) * shear
                if not first:
                    new0 = stress[0, j, at, :] + new0
                    new1 = stress[1, j, at, :] + new1
                    new2 = stress[2, j, at, :] + new2
                stress[0, j, at, :] = new0 * covered
                stress[1, j, at, :] = new1 * covered
                stress[2, j, at, :] = new2 * covered

    def velocity_step():
        @pl.loop(0, all_strips)
        def _(i):
            at, up, down = strip_rows(i, 0), strip_rows(i, -1), strip_rows(i, 1)
            first = rows_of(stress, 0, at)
            second = rows_of(stress, 1, at)
            east_normal = sides([0.5 * (a + b) for a, b in zip(first, second)])
            east_third = sides(rows_of(stress, 2, at))
            for j in range(every):
                north_third = 0.5 * (stress[2, j, down, :] - stress[2, j, up, :])
                north_normal = 0.25 * (
                    (stress[0, j, down, :] - stress[1, j, down, :])
                    - (stress[0, j, up, :] - stress[1, j, up, :])
                )
                u, v = fields[U, j, at, :], fields[V, j, at, :]
                cx, cy = surf[0, j, at, :], surf[1, j, at, :]
                mass = fields[THICK, j, at, :]
                rel_u, rel_v = cx - u, cy - v
                drag = 0.8 * jnp.sqrt(rel_u * rel_u + rel_v * rel_v)
                a = mass + drag
                b = 0.5 * mass
                rx = mass * u + (east_normal[j] + north_third) + drag * cx + fields[WX, j, at, :]
                ry = mass * v + (east_third[j] + north_normal) + drag * cy + fields[WY, j, at, :]
                live = fields[MOVING, j, at, :] > 0.5
                inverse = 1.0 / jnp.where(live, a * a + b * b, 1.0)
                fields[U, j, at, :] = jnp.where(live, (a * rx + b * ry) * inverse, 0.0)
                fields[V, j, at, :] = jnp.where(live, (a * ry - b * rx) * inverse, 0.0)

    stress_step(True)

    for pair in z_copies:
        for copy in pair:
            copy.wait_recv()
    norm = 1.0 / math.sqrt(levels)
    for c in range(3):
        scales = [twice(z_recv_scale[k, c]) for k in range(rows_g - 1)]

        @pl.loop(0, strips)
        def _(i, c=c, scales=scales):
            at = pl.ds(pl.multiple_of(i * 16, 16), 16)
            to = pl.ds(pl.multiple_of(i * 16 + top, 8), 16)
            for j in range(tiles):
                value = own[c, at, pl.ds(j * LANES, LANES)]
                for k in range(rows_g - 1):
                    value = value + decoded(z_recv.at[k, c], scales[k], at, j)
                surf[c, j, to, :] = value * norm

    for copy in send_rows(surf, ns_surf, ns_sems.at[1]):
        copy.wait()
    place_rows(surf, ns_surf, 3)
    for copy in send_columns(surf, ew_surf, ew_sems.at[1]):
        copy.wait()
    place_columns(surf, ew_surf, 3)

    @pl.loop(0, all_strips)
    def _(i):
        at, up, down = strip_rows(i, 0), strip_rows(i, -1), strip_rows(i, 1)
        slope_x = sides(rows_of(surf, 2, at))
        for j in range(every):
            slope_y = 0.5 * (surf[2, j, down, :] - surf[2, j, up, :])
            gain = -0.5 * fields[THICK, j, at, :]
            fields[WX, j, at, :] = fields[WX, j, at, :] + gain * slope_x[j]
            fields[WY, j, at, :] = fields[WY, j, at, :] + gain * slope_y

    velocity_step()

    @pl.loop(0, SUB - 2)
    def _(cycle):
        stress_step(False)
        velocity_step()

    stress_step(False)
    outs = []
    rows = pl.ds(top, tile_rows)
    for j in range(tiles):
        copy = pltpu.make_async_copy(
            stress.at[:, j, rows, :], stress_out.at[:, :, pl.ds(j * LANES, LANES)], out_sem.at[0, j]
        )
        copy.start()
        outs.append(copy)
    velocity_step()
    for j in range(tiles):
        copy = pltpu.make_async_copy(
            fields.at[pl.ds(U, 2), j, rows, :],
            vel_out.at[:, :, pl.ds(j * LANES, LANES)],
            out_sem.at[1, j],
        )
        copy.start()
        outs.append(copy)
    for copy in outs:
        copy.wait()
    for pair in list(y_copies.values()) + z_copies:
        for copy in pair:
            copy.wait_send()


def body(
    ocean, level_weight, velocity_start, wind_stress, thickness, concentration, ice_mask, land_mask
):
    secs, rows_g, cols_g = lax.axis_size("sec"), lax.axis_size("gy"), lax.axis_size("gx")
    held = ocean.shape[0]
    rows, cols = thickness.shape
    tiles = cols // LANES
    tall = rows + 4 * HALO
    wide_rows = rows + 2 * HALO
    f32, i16 = jnp.float32, jnp.int16
    dma = pltpu.SemaphoreType.DMA
    y_slots = (secs - 1) * rows_g
    z_slots = rows_g - 1
    anywhere = pl.BlockSpec(memory_space=pl.ANY)
    return pl.pallas_call(
        functools.partial(kernel, (secs, rows_g, cols_g, level_weight.shape[0])),
        out_shape=(
            jax.ShapeDtypeStruct((2, rows, cols), f32),
            jax.ShapeDtypeStruct((3, rows, cols), f32),
        ),
        in_specs=[pl.BlockSpec(memory_space=pltpu.SMEM)] + [anywhere] * 7,
        out_specs=(anywhere, anywhere),
        scratch_shapes=[
            pltpu.VMEM((secs * rows_g, held, 3, rows, cols), ocean.dtype),
            pltpu.VMEM((rows, cols), f32),
            pltpu.VMEM((y_slots, 3, rows, cols), i16),
            pltpu.VMEM((y_slots, 3, rows, cols), i16),
            pltpu.VMEM((y_slots, 3, 8, LANES), f32),
            pltpu.VMEM((y_slots, 3, 8, LANES), f32),
            pltpu.VMEM((z_slots, 3, rows, cols), i16),
            pltpu.VMEM((z_slots, 3, rows, cols), i16),
            pltpu.VMEM((z_slots, 3, 8, LANES), f32),
            pltpu.VMEM((z_slots, 3, 8, LANES), f32),
            pltpu.VMEM((3, rows, cols), f32),
            pltpu.VMEM((2, tiles, rows, LANES), jnp.int32),
            pltpu.VMEM((FIELDS, tiles + 1, tall, LANES), f32),
            pltpu.VMEM((3, tiles + 1, tall, LANES), f32),
            pltpu.VMEM((3, tiles + 1, tall, LANES), f32),
            pltpu.VMEM((2, FIELDS, tiles, HALO, LANES), f32),
            pltpu.VMEM((2, FIELDS, wide_rows, LANES), f32),
            pltpu.VMEM((2, 3, tiles, HALO, LANES), f32),
            pltpu.VMEM((2, 3, wide_rows, LANES), f32),
            dma((secs * rows_g,)),
            dma((tiles, 6)),
            dma((y_slots, 3, 2, 2)),
            dma((z_slots, 3, 2, 2)),
            dma((2, 2, 2)),
            dma((2, 2, 2)),
            dma((2, tiles)),
        ],
        compiler_params=pltpu.CompilerParams(
            collective_id=0, has_side_effects=True, vmem_limit_bytes=60 * 1024 * 1024
        ),
    )(
        level_weight,
        ocean,
        velocity_start,
        wind_stress,
        thickness,
        concentration,
        ice_mask,
        land_mask,
    )


def solution(mesh):
    placed = (
        P(("sec", "gy"), None, None, "gx"),
        P(),
        P(None, ("sec", "gy"), "gx"),
        P(None, ("sec", "gy"), "gx"),
        P(("sec", "gy"), "gx"),
        P(("sec", "gy"), "gx"),
        P(("sec", "gy"), "gx"),
        P(("sec", "gy"), "gx"),
    )
    return jax.shard_map(
        body,
        mesh=mesh,
        in_specs=placed,
        out_specs=(P(None, ("sec", "gy"), "gx"), P(None, ("sec", "gy"), "gx")),
        check_vma=False,
    )
```

time: 327 us -> 70.1 us (0.21); the launches traced: 323 us -> 69.9 us
  waiting for transfers between devices: 163 us -> 0 us
  Pallas kernels: 0 us -> 65.6 us
  starting transfers between devices: 63.3 us -> 0 us
  other arithmetic: 40.6 us -> 0 us
  local copies, waits for them, and re-layouts: 40.9 us -> 3.68 us
  between operations: 14.7 us -> 0.64 us
    ppermute x36 -> x0, waiting for transfers between devices: 117 us -> none  [the longest x18 90.4 us: from_behind(): lax.ppermute(value, axis, [(source, source + steps) for source in range(l...]
    pallas_call x0 -> x1, Pallas kernels: none -> 65.6 us  [body(): pl.pallas_call(functools.partial(kernel, (secs, rows_g, cols_g, level_wei...]
    ppermute x36 -> x0, starting transfers between devices: 63.3 us -> none  [the longest x18 50 us: from_behind(): lax.ppermute(value, axis, [(source, source + steps) for source in range(l...]
    reduce_scatter x1 -> x0, waiting for transfers between devices: 46.1 us -> none  [body(): lax.psum_scatter(jnp.transpose(summed, (1, 0, 2)).reshape(tile_rows * lax...]
    add x4 -> x0, other arithmetic: 24.9 us -> none  [add_held(): return total + own_weights[level] * ocean[level].astype(jnp.float32)]
    slice x25 -> x0, local copies, waits for them, and re-layouts: 16.4 us -> none  [the longest x13 11.5 us: extend(): lower = from_behind(wide[:, -width:, :], ('sec', 'gy'), 1)]
    ppermute x8 -> x0, local copies, waits for them, and re-layouts: 9.32 us -> none  [from_behind(): lax.ppermute(value, axis, [(source, source + steps) for source in range(l...]
    concatenate x17 -> x0, other arithmetic: 7.82 us -> none  [the longest x8 7.49 us: extend(): return jnp.concatenate([lower, wide, upper], axis=1)]
  transfers between devices with their start and end apart: 37 -> 0, of which waited for: 33 -> 0; matrix products, arithmetic and copies ran while one was open for 6% -> 0% of each run, Pallas kernels for 0% -> 0%
where the time goes in v1:
time: 70.1 us; the launch traced here: 69.9 us
  Pallas kernels  65.6 us (94%)
  local copies, waits for them, and re-layouts  3.68 us (5%)
    pallas_call x1, Pallas kernels, body(): pl.pallas_call(functools.partial(kernel, (secs, rows_g, cols_g, level_wei...  65.6 us
    unnamed x2, local copies, waits for them, and re-layouts  3.68 us

profile of v1, /device:TPU:25, one launch (start us, length us, event | category | flops | bytes accessed | tf_op | source)
XLA Modules:
  0.0 69.9 jit_solution(17274320782225777358)
XLA Ops:
  0.6 65.6 %shard_map.95 = (f32[2,128,384]{2,1,0:T(8,128)}, f32[3,128,384]{2,1,0:T(8,128)}) custom-call(f32[32]{0:T(128)} %weight_ref.1, bf16[4,3,1024,384]{3,2,1,0:T(8,128)(2,1)} %ocean_hbm.1, f32[2,128,384]{2,1,0:T(8,128)} %vel_hbm.1, f32[2,128,384]{2,1,0:T(8,128)} %wind_hbm.1, f32[128,384]{1,0:T(8,128)} %thick_hbm.1, f32[128,384]{1,0:T(8,128)} %conc_hbm.1, ...), custom_call_target="tpu_custom_call" | custom-call | tf_op jit(solution)/shard_map/pallas_call | solution.py:470
  66.2 1.8 %copy.12 = f32[2,128,384]{2,1,0:T(8,128)} copy(f32[2,128,384]{2,1,0:T(8,128)} %get-tuple-element.4) | data formatting | bytes 786432
  68.0 1.9 %copy.13 = f32[3,128,384]{2,1,0:T(8,128)} copy(f32[3,128,384]{2,1,0:T(8,128)} %get-tuple-element.5) | data formatting | bytes 1179648

commit v2 on v1

--- a/solution.py
+++ b/solution.py
@@ -10,6 +10,7 @@
 
 SUB = 4
 HALO = 8
+VMEM_OUT = 8 * 1024 * 1024
 LANES = 128
 MESH = pl.DeviceIdType.MESH
 
@@ -27,8 +28,8 @@
     conc_hbm,
     ice_hbm,
     land_hbm,
-    vel_out,
-    stress_out,
+    fields,
+    stress,
     ocean,
     total,
     y_send,
@@ -41,20 +42,20 @@
     z_recv_scale,
     own,
     masks,
-    fields,
-    stress,
     surf,
     ns_field,
     ew_field,
     ns_surf,
-    ew_surf,
+    side_send,
+    side_recv,
+    corner_recv,
     ocean_sem,
     static_sem,
     y_sems,
     z_sems,
     ns_sems,
     ew_sems,
-    out_sem,
+    surf_sems,
 ):
     secs, rows_g, cols_g, levels = dims
     held = ocean_hbm.shape[0]
@@ -73,6 +74,8 @@
     north, south = at_rank(rank - 1), at_rank(rank + 1)
     west = (s, g, lax.rem(x + cols_g - 1, cols_g))
     east = (s, g, lax.rem(x + 1, cols_g))
+    north_west, north_east = north[:2] + west[2:], north[:2] + east[2:]
+    south_west, south_east = south[:2] + west[2:], south[:2] + east[2:]
     over_secs = [(lax.rem(s + i, secs), g, x) for i in range(1, secs)]
     over_rows = [(s, lax.rem(g + k, rows_g), x) for k in range(1, rows_g)]
 
@@ -111,6 +114,7 @@
 
     barrier = pltpu.get_barrier_semaphore()
     partners = over_secs + over_rows + [north, south, west, east]
+    partners += [north_west, north_east, south_west, south_east]
     for partner in partners:
         pl.semaphore_signal(barrier, inc=1, device_id=partner, device_id_type=MESH)
     pl.semaphore_wait(barrier, len(partners))
@@ -147,12 +151,14 @@
                 most = jnp.maximum(most, jnp.abs(value))
             return most
 
-        most = lax.fori_loop(0, strips, first, jnp.zeros((16, LANES), jnp.float32))
+        most = lax.fori_loop(
+            0, strips, first, jnp.zeros((16, LANES), jnp.float32), unroll=True
+        )
         most = jnp.maximum(jnp.maximum(most[0:8], most[8:16]), 1e-30)
         scale_ref[...] = most * (1.0 / 32767.0)
         inverse = twice(32767.0 / most)
 
-        @pl.loop(0, strips)
+        @pl.loop(0, strips, unroll=True)
         def _(i):
             at = pl.ds(pl.multiple_of(i * 16, 16), 16)
             for j in range(tiles):
@@ -247,7 +253,7 @@
                     jnp.where(lane >= LANES - HALO, received[0, f, at, :], 0.0),
                 )
 
-    field_rows = send_rows(fields, ns_field, ns_sems.at[0])
+    field_rows = send_rows(fields, ns_field, ns_sems)
 
     z_copies = []
     field_columns = None
@@ -268,7 +274,7 @@
 
             if k == 0:
 
-                @pl.loop(0, strips)
+                @pl.loop(0, strips, unroll=True)
                 def _(i, value_of=value_of, c=c):
                     at = pl.ds(pl.multiple_of(i * 16, 16), 16)
                     for j in range(tiles):
@@ -292,7 +298,7 @@
             for copy in field_rows:
                 copy.wait()
             place_rows(fields, ns_field, FIELDS)
-            field_columns = send_columns(fields, ew_field, ew_sems.at[0])
+            field_columns = send_columns(fields, ew_field, ew_sems)
 
     for copy in field_columns:
         copy.wait()
@@ -329,7 +335,7 @@
         return [ref[f, j, at, :] for j in range(every)]
 
     def stress_step(first):
-        @pl.loop(0, all_strips)
+        @pl.loop(0, all_strips, unroll=6)
         def _(i):
             at, up, down = strip_rows(i, 0), strip_rows(i, -1), strip_rows(i, 1)
             east_u = sides(rows_of(fields, U, at))
@@ -358,7 +364,7 @@
                 stress[2, j, at, :] = new2 * covered
 
     def velocity_step():
-        @pl.loop(0, all_strips)
+        @pl.loop(0, all_strips, unroll=6)
         def _(i):
             at, up, down = strip_rows(i, 0), strip_rows(i, -1), strip_rows(i, 1)
             first = rows_of(stress, 0, at)
@@ -387,14 +393,17 @@
 
     stress_step(True)
 
-    for pair in z_copies:
-        for copy in pair:
-            copy.wait_recv()
     norm = 1.0 / math.sqrt(levels)
+    tile_strips = tile_rows // 8
+    per_piece = LANES // HALO
+    halo_copies = []
     for c in range(3):
+        for k in range(rows_g - 1):
+            for copy in z_copies[k * 3 + c]:
+                copy.wait_recv()
         scales = [twice(z_recv_scale[k, c]) for k in range(rows_g - 1)]
 
-        @pl.loop(0, strips)
+        @pl.loop(0, strips, unroll=True)
         def _(i, c=c, scales=scales):
             at = pl.ds(pl.multiple_of(i * 16, 16), 16)
             to = pl.ds(pl.multiple_of(i * 16 + top, 8), 16)
@@ -404,14 +413,61 @@
                     value = value + decoded(z_recv.at[k, c], scales[k], at, j)
                 surf[c, j, to, :] = value * norm
 
-    for copy in send_rows(surf, ns_surf, ns_sems.at[1]):
-        copy.wait()
-    place_rows(surf, ns_surf, 3)
-    for copy in send_columns(surf, ew_surf, ew_sems.at[1]):
-        copy.wait()
-    place_columns(surf, ew_surf, 3)
-
-    @pl.loop(0, all_strips)
+        for side, j, offset in ((0, 0, 0), (1, tiles - 1, HALO)):
+            for piece in range(-(-tile_strips // per_piece)):
+                packed = jnp.zeros((8, LANES), jnp.float32)
+                for q in range(min(per_piece, tile_strips - piece * per_piece)):
+                    value = surf[c, j, pl.ds(top + 8 * (piece * per_piece + q), 8), :]
+                    shift = (q * HALO + offset) % LANES
+                    value = pltpu.roll(value, shift, 1) if shift else value
+                    packed = jnp.where(lane // HALO == q, value, packed)
+                side_send[c, side, piece] = packed
+        first, last = pl.ds(top, HALO), pl.ds(end - HALO, HALO)
+        copies = []
+        for n, (source, target, device) in enumerate(
+            (
+                (surf.at[c, inner, first, :], ns_surf.at[1, c], north),
+                (surf.at[c, inner, last, :], ns_surf.at[0, c], south),
+                (side_send.at[c, 0], side_recv.at[c, 1], west),
+                (side_send.at[c, 1], side_recv.at[c, 0], east),
+                (surf.at[c, 0, first, :], corner_recv.at[c, 3], north_west),
+                (surf.at[c, tiles - 1, first, :], corner_recv.at[c, 2], north_east),
+                (surf.at[c, 0, last, :], corner_recv.at[c, 1], south_west),
+                (surf.at[c, tiles - 1, last, :], corner_recv.at[c, 0], south_east),
+            )
+        ):
+            copy = remote(source, target, surf_sems.at[c, n], device)
+            copy.start()
+            copies.append(copy)
+        halo_copies.append(copies)
+
+    above = jnp.where(rank > 0, 1.0, 0.0)
+    below = jnp.where(rank < ranks - 1, 1.0, 0.0)
+    for c in range(3):
+        for copy in halo_copies[c]:
+            copy.wait()
+        for j in range(tiles):
+            surf[c, j, pl.ds(HALO, HALO), :] = ns_surf[0, c, j] * above
+            surf[c, j, pl.ds(end, HALO), :] = ns_surf[1, c, j] * below
+
+        def beyond(west_value, east_value):
+            return jnp.where(
+                lane < HALO, east_value, jnp.where(lane >= LANES - HALO, west_value, 0.0)
+            )
+
+        surf[c, tiles, pl.ds(HALO, HALO), :] = above * beyond(corner_recv[c, 0], corner_recv[c, 1])
+        surf[c, tiles, pl.ds(end, HALO), :] = below * beyond(corner_recv[c, 2], corner_recv[c, 3])
+        for t in range(tile_strips):
+            piece, q = divmod(t, per_piece)
+            from_west = side_recv[c, 0, piece]
+            from_east = side_recv[c, 1, piece]
+            back = (LANES - HALO - q * HALO) % LANES
+            from_west = pltpu.roll(from_west, back, 1) if back else from_west
+            back = (LANES - q * HALO) % LANES
+            from_east = pltpu.roll(from_east, back, 1) if back else from_east
+            surf[c, tiles, pl.ds(top + 8 * t, 8), :] = beyond(from_west, from_east)
+
+    @pl.loop(0, all_strips, unroll=6)
     def _(i):
         at, up, down = strip_rows(i, 0), strip_rows(i, -1), strip_rows(i, 1)
         slope_x = sides(rows_of(surf, 2, at))
@@ -429,28 +485,28 @@
         velocity_step()
 
     stress_step(False)
-    outs = []
-    rows = pl.ds(top, tile_rows)
-    for j in range(tiles):
-        copy = pltpu.make_async_copy(
-            stress.at[:, j, rows, :], stress_out.at[:, :, pl.ds(j * LANES, LANES)], out_sem.at[0, j]
-        )
-        copy.start()
-        outs.append(copy)
     velocity_step()
-    for j in range(tiles):
-        copy = pltpu.make_async_copy(
-            fields.at[pl.ds(U, 2), j, rows, :],
-            vel_out.at[:, :, pl.ds(j * LANES, LANES)],
-            out_sem.at[1, j],
-        )
-        copy.start()
-        outs.append(copy)
-    for copy in outs:
-        copy.wait()
     for pair in list(y_copies.values()) + z_copies:
         for copy in pair:
             copy.wait_send()
+
+
+def write_out(fields, stress, vel_out, stress_out, sems):
+    tiles = fields.shape[1] - 1
+    rows = pl.ds(2 * HALO, vel_out.shape[1])
+    copies = []
+    for j in range(tiles):
+        cols = pl.ds(j * LANES, LANES)
+        for n, (source, target) in enumerate(
+            ((fields.at[pl.ds(U, 2)], vel_out), (stress, stress_out))
+        ):
+            copy = pltpu.make_async_copy(
+                source.at[:, j, rows, :], target.at[:, :, cols], sems.at[n, j]
+            )
+            copy.start()
+            copies.append(copy)
+    for copy in copies:
+        copy.wait()
 
 
 def body(
@@ -462,19 +518,21 @@
     tiles = cols // LANES
     tall = rows + 4 * HALO
     wide_rows = rows + 2 * HALO
+    pieces = pl.cdiv(rows, LANES)
     f32, i16 = jnp.float32, jnp.int16
     dma = pltpu.SemaphoreType.DMA
     y_slots = (secs - 1) * rows_g
     z_slots = rows_g - 1
     anywhere = pl.BlockSpec(memory_space=pl.ANY)
-    return pl.pallas_call(
+    on_chip = pl.BlockSpec(memory_space=pltpu.VMEM)
+    fields, stress = pl.pallas_call(
         functools.partial(kernel, (secs, rows_g, cols_g, level_weight.shape[0])),
         out_shape=(
-            jax.ShapeDtypeStruct((2, rows, cols), f32),
-            jax.ShapeDtypeStruct((3, rows, cols), f32),
+            pltpu.VMEM((FIELDS, tiles + 1, tall, LANES), f32),
+            pltpu.VMEM((3, tiles + 1, tall, LANES), f32),
         ),
         in_specs=[pl.BlockSpec(memory_space=pltpu.SMEM)] + [anywhere] * 7,
-        out_specs=(anywhere, anywhere),
+        out_specs=(on_chip, on_chip),
         scratch_shapes=[
             pltpu.VMEM((secs * rows_g, held, 3, rows, cols), ocean.dtype),
             pltpu.VMEM((rows, cols), f32),
@@ -488,23 +546,23 @@
             pltpu.VMEM((z_slots, 3, 8, LANES), f32),
             pltpu.VMEM((3, rows, cols), f32),
             pltpu.VMEM((2, tiles, rows, LANES), jnp.int32),
-            pltpu.VMEM((FIELDS, tiles + 1, tall, LANES), f32),
-            pltpu.VMEM((3, tiles + 1, tall, LANES), f32),
             pltpu.VMEM((3, tiles + 1, tall, LANES), f32),
             pltpu.VMEM((2, FIELDS, tiles, HALO, LANES), f32),
             pltpu.VMEM((2, FIELDS, wide_rows, LANES), f32),
             pltpu.VMEM((2, 3, tiles, HALO, LANES), f32),
-            pltpu.VMEM((2, 3, wide_rows, LANES), f32),
+            pltpu.VMEM((3, 2, pieces, 8, LANES), f32),
+            pltpu.VMEM((3, 2, pieces, 8, LANES), f32),
+            pltpu.VMEM((3, 4, HALO, LANES), f32),
             dma((secs * rows_g,)),
             dma((tiles, 6)),
             dma((y_slots, 3, 2, 2)),
             dma((z_slots, 3, 2, 2)),
-            dma((2, 2, 2)),
-            dma((2, 2, 2)),
-            dma((2, tiles)),
+            dma((2, 2)),
+            dma((2, 2)),
+            dma((3, 8, 2)),
         ],
         compiler_params=pltpu.CompilerParams(
-            collective_id=0, has_side_effects=True, vmem_limit_bytes=60 * 1024 * 1024
+            collective_id=0, has_side_effects=True, vmem_limit_bytes=52 * 1024 * 1024
         ),
     )(
         level_weight,
@@ -516,6 +574,17 @@
         ice_mask,
         land_mask,
     )
+    return pl.pallas_call(
+        write_out,
+        out_shape=(
+            jax.ShapeDtypeStruct((2, rows, cols), f32),
+            jax.ShapeDtypeStruct((3, rows, cols), f32),
+        ),
+        in_specs=[on_chip, on_chip],
+        out_specs=(anywhere, anywhere),
+        scratch_shapes=[dma((2, tiles))],
+        compiler_params=pltpu.CompilerParams(vmem_limit_bytes=VMEM_OUT),
+    )(fields, stress)
 
 
 def solution(mesh):

time: 70.1 us -> 53.8 us (0.77)
  Pallas kernels: 65.6 us -> 52.3 us
  local copies, waits for them, and re-layouts: 3.68 us -> 0 us
    pallas_call x1, Pallas kernels: 65.6 us -> 51.3 us  [body(): pl.pallas_call(functools.partial(kernel, (secs, rows_g, cols_g, level_wei...]
    unnamed x2 -> x0, local copies, waits for them, and re-layouts: 3.68 us -> none
    pallas_call x0 -> x1, Pallas kernels: none -> 0.99 us  [body(): pl.pallas_call(write_out, out_shape=(jax.ShapeDtypeStruct((2, rows, cols)...]
where the time goes in v2:
time: 53.8 us; the launch traced here: 53 us
  Pallas kernels  52.3 us (97%)
  between operations  0.64 us (1%)
    pallas_call x1, Pallas kernels, body(): pl.pallas_call(functools.partial(kernel, (secs, rows_g, cols_g, level_wei...  51.3 us

profile of v2, /device:TPU:25, one launch (start us, length us, event | category | flops | bytes accessed | tf_op | source)
XLA Modules:
  0.0 53.0 jit_solution(3577706171888398054)
XLA Ops:
  0.6 51.3 %shard_map.95 = (f32[8,4,160,128]{3,2,1,0:T(8,128)S(1)}, f32[3,4,160,128]{3,2,1,0:T(8,128)S(1)}) custom-call(f32[32]{0:T(128)} %weight_ref.1, bf16[4,3,1024,384]{3,2,1,0:T(8,128)(2,1)} %ocean_hbm.1, f32[2,128,384]{2,1,0:T(8,128)} %vel_hbm.1, f32[2,128,384]{2,1,0:T(8,128)} %wind_hbm.1, f32[128,384]{1,0:T(8,128)} %thick_hbm.1, f32[128,384]{1,0:T(8,128)} %conc_hbm.1, ...), custom_call_target="tpu_custom_call" | custom-call | tf_op jit(solution)/shard_map/pallas_call | solution.py:528
  52.0 1.0 %shard_map.96 = (f32[2,128,384]{2,1,0:T(8,128)}, f32[3,128,384]{2,1,0:T(8,128)}) custom-call(f32[8,4,160,128]{3,2,1,0:T(8,128)S(1)} %get-tuple-element.4.fields, f32[3,4,160,128]{3,2,1,0:T(8,128)S(1)} %get-tuple-element.5.stress), custom_call_target="tpu_custom_call" | custom-call | tf_op jit(solution)/shard_map/pallas_call | solution.py:577

commit v3 on v2

--- a/solution.py
+++ b/solution.py
@@ -40,7 +40,6 @@
     z_recv,
     z_send_scale,
     z_recv_scale,
-    own,
     masks,
     surf,
     ns_field,
@@ -80,6 +79,12 @@
     over_rows = [(s, lax.rem(g + k, rows_g), x) for k in range(1, rows_g)]
 
     order = [rows_g // 2] + [k for k in range(1, rows_g) if k != rows_g // 2] + [0]
+
+    barrier = pltpu.get_barrier_semaphore()
+    partners = over_secs + over_rows + [north, south, west, east]
+    partners += [north_west, north_east, south_west, south_east]
+    for partner in partners:
+        pl.semaphore_signal(barrier, inc=1, device_id=partner, device_id_type=MESH)
 
     def block_rows(sec, k):
         block = sec * rows_g + lax.rem(g + k, rows_g)
@@ -112,13 +117,6 @@
             copy.start()
             static_copies.append(copy)
 
-    barrier = pltpu.get_barrier_semaphore()
-    partners = over_secs + over_rows + [north, south, west, east]
-    partners += [north_west, north_east, south_west, south_east]
-    for partner in partners:
-        pl.semaphore_signal(barrier, inc=1, device_id=partner, device_id_type=MESH)
-    pl.semaphore_wait(barrier, len(partners))
-
     def remote(source, target, sems, device):
         return pltpu.make_async_remote_copy(
             src_ref=source,
@@ -134,6 +132,7 @@
 
     def level_sum(slot, c, at, j):
         cols = pl.ds(j * LANES, LANES)
+        c = (c + 2) % 3
         value = own_weights[0] * ocean[slot, 0, c, at, cols].astype(jnp.float32)
         for k in range(1, held):
             value = value + own_weights[k] * ocean[slot, k, c, at, cols].astype(jnp.float32)
@@ -181,6 +180,8 @@
                     y_send.at[slot],
                     y_send_scale.at[slot],
                 )
+                if not y_copies:
+                    pl.semaphore_wait(barrier, len(partners))
                 pair = (
                     remote(y_send.at[slot], y_recv.at[slot], y_sems.at[slot + (0,)], over_secs[i - 1]),
                     remote(
@@ -255,54 +256,6 @@
 
     field_rows = send_rows(fields, ns_field, ns_sems)
 
-    z_copies = []
-    field_columns = None
-    for k in order:
-        ocean_copies[0, k].wait()
-        for c in range(3):
-            slots = [((i - 1) * rows_g + k, c) for i in range(1, secs)]
-            for i in range(1, secs):
-                for copy in y_copies[i, k, c]:
-                    copy.wait_recv()
-            scales = [twice(y_recv_scale[slot]) for slot in slots]
-
-            def value_of(at, j, k=k, c=c, slots=slots, scales=scales):
-                value = level_sum(k, c, at, j)
-                for slot, scale in zip(slots, scales):
-                    value = value + decoded(y_recv.at[slot], scale, at, j)
-                return value
-
-            if k == 0:
-
-                @pl.loop(0, strips, unroll=True)
-                def _(i, value_of=value_of, c=c):
-                    at = pl.ds(pl.multiple_of(i * 16, 16), 16)
-                    for j in range(tiles):
-                        own[c, at, pl.ds(j * LANES, LANES)] = value_of(at, j)
-            else:
-                slot = (k - 1, c)
-                coded(value_of, z_send.at[slot], z_send_scale.at[slot])
-                pair = (
-                    remote(z_send.at[slot], z_recv.at[slot], z_sems.at[slot + (0,)], over_rows[k - 1]),
-                    remote(
-                        z_send_scale.at[slot],
-                        z_recv_scale.at[slot],
-                        z_sems.at[slot + (1,)],
-                        over_rows[k - 1],
-                    ),
-                )
-                for copy in pair:
-                    copy.start()
-                z_copies.append(pair)
-        if k == order[0]:
-            for copy in field_rows:
-                copy.wait()
-            place_rows(fields, ns_field, FIELDS)
-            field_columns = send_columns(fields, ew_field, ew_sems)
-
-    for copy in field_columns:
-        copy.wait()
-    place_columns(fields, ew_field, FIELDS)
     every = tiles + 1
 
     def margins(target, count):
@@ -311,10 +264,6 @@
             for j in range(every):
                 target[f, j, pl.ds(0, HALO), :] = zero
                 target[f, j, pl.ds(end + HALO, HALO), :] = zero
-
-    margins(fields, 2)
-    margins(stress, 3)
-    margins(surf, 3)
 
     def sides(values):
         before = [pltpu.roll(value, 1, 1) for value in values]
@@ -335,7 +284,7 @@
         return [ref[f, j, at, :] for j in range(every)]
 
     def stress_step(first):
-        @pl.loop(0, all_strips, unroll=6)
+        @pl.loop(0, all_strips, unroll=True)
         def _(i):
             at, up, down = strip_rows(i, 0), strip_rows(i, -1), strip_rows(i, 1)
             east_u = sides(rows_of(fields, U, at))
@@ -363,22 +312,22 @@
                 stress[1, j, at, :] = new1 * covered
                 stress[2, j, at, :] = new2 * covered
 
-    def velocity_step():
-        @pl.loop(0, all_strips, unroll=6)
+    def velocity_step(first_strip=0, last_strip=all_strips, width=tiles + 1):
+        @pl.loop(first_strip, last_strip, unroll=True)
         def _(i):
             at, up, down = strip_rows(i, 0), strip_rows(i, -1), strip_rows(i, 1)
             first = rows_of(stress, 0, at)
             second = rows_of(stress, 1, at)
             east_normal = sides([0.5 * (a + b) for a, b in zip(first, second)])
             east_third = sides(rows_of(stress, 2, at))
-            for j in range(every):
+            for j in range(width):
                 north_third = 0.5 * (stress[2, j, down, :] - stress[2, j, up, :])
                 north_normal = 0.25 * (
                     (stress[0, j, down, :] - stress[1, j, down, :])
                     - (stress[0, j, up, :] - stress[1, j, up, :])
                 )
                 u, v = fields[U, j, at, :], fields[V, j, at, :]
-                cx, cy = surf[0, j, at, :], surf[1, j, at, :]
+                cx, cy = surf[1, j, at, :], surf[2, j, at, :]
                 mass = fields[THICK, j, at, :]
                 rel_u, rel_v = cx - u, cy - v
                 drag = 0.8 * jnp.sqrt(rel_u * rel_u + rel_v * rel_v)
@@ -391,24 +340,22 @@
                 fields[U, j, at, :] = jnp.where(live, (a * rx + b * ry) * inverse, 0.0)
                 fields[V, j, at, :] = jnp.where(live, (a * ry - b * rx) * inverse, 0.0)
 
-    stress_step(True)
-
     norm = 1.0 / math.sqrt(levels)
     tile_strips = tile_rows // 8
     per_piece = LANES // HALO
     halo_copies = []
-    for c in range(3):
+    def surface_of(c, value_of):
         for k in range(rows_g - 1):
             for copy in z_copies[k * 3 + c]:
                 copy.wait_recv()
         scales = [twice(z_recv_scale[k, c]) for k in range(rows_g - 1)]
 
         @pl.loop(0, strips, unroll=True)
-        def _(i, c=c, scales=scales):
+        def _(i):
             at = pl.ds(pl.multiple_of(i * 16, 16), 16)
             to = pl.ds(pl.multiple_of(i * 16 + top, 8), 16)
             for j in range(tiles):
-                value = own[c, at, pl.ds(j * LANES, LANES)]
+                value = value_of(at, j)
                 for k in range(rows_g - 1):
                     value = value + decoded(z_recv.at[k, c], scales[k], at, j)
                 surf[c, j, to, :] = value * norm
@@ -441,6 +388,54 @@
             copies.append(copy)
         halo_copies.append(copies)
 
+    z_copies = []
+    field_columns = None
+    for k in order:
+        ocean_copies[0, k].wait()
+        for c in range(3):
+            slots = [((i - 1) * rows_g + k, c) for i in range(1, secs)]
+            for i in range(1, secs):
+                for copy in y_copies[i, k, c]:
+                    copy.wait_recv()
+            scales = [twice(y_recv_scale[slot]) for slot in slots]
+
+            def value_of(at, j, k=k, c=c, slots=slots, scales=scales):
+                value = level_sum(k, c, at, j)
+                for slot, scale in zip(slots, scales):
+                    value = value + decoded(y_recv.at[slot], scale, at, j)
+                return value
+
+            if k == 0:
+                surface_of(c, value_of)
+                if c == 0:
+                    for copy in field_columns:
+                        copy.wait()
+                    place_columns(fields, ew_field, FIELDS)
+                    margins(fields, 2)
+                    margins(stress, 3)
+                    margins(surf, 3)
+                    stress_step(True)
+            else:
+                slot = (k - 1, c)
+                coded(value_of, z_send.at[slot], z_send_scale.at[slot])
+                pair = (
+                    remote(z_send.at[slot], z_recv.at[slot], z_sems.at[slot + (0,)], over_rows[k - 1]),
+                    remote(
+                        z_send_scale.at[slot],
+                        z_recv_scale.at[slot],
+                        z_sems.at[slot + (1,)],
+                        over_rows[k - 1],
+                    ),
+                )
+                for copy in pair:
+                    copy.start()
+                z_copies.append(pair)
+        if k == order[0]:
+            for copy in field_rows:
+                copy.wait()
+            place_rows(fields, ns_field, FIELDS)
+            field_columns = send_columns(fields, ew_field, ew_sems)
+
     above = jnp.where(rank > 0, 1.0, 0.0)
     below = jnp.where(rank < ranks - 1, 1.0, 0.0)
     for c in range(3):
@@ -466,16 +461,17 @@
             back = (LANES - q * HALO) % LANES
             from_east = pltpu.roll(from_east, back, 1) if back else from_east
             surf[c, tiles, pl.ds(top + 8 * t, 8), :] = beyond(from_west, from_east)
-
-    @pl.loop(0, all_strips, unroll=6)
-    def _(i):
-        at, up, down = strip_rows(i, 0), strip_rows(i, -1), strip_rows(i, 1)
-        slope_x = sides(rows_of(surf, 2, at))
-        for j in range(every):
-            slope_y = 0.5 * (surf[2, j, down, :] - surf[2, j, up, :])
-            gain = -0.5 * fields[THICK, j, at, :]
-            fields[WX, j, at, :] = fields[WX, j, at, :] + gain * slope_x[j]
-            fields[WY, j, at, :] = fields[WY, j, at, :] + gain * slope_y
+        if c == 0:
+
+            @pl.loop(0, all_strips, unroll=True)
+            def _(i):
+                at, up, down = strip_rows(i, 0), strip_rows(i, -1), strip_rows(i, 1)
+                slope_x = sides(rows_of(surf, 0, at))
+                for j in range(every):
+                    slope_y = 0.5 * (surf[0, j, down, :] - surf[0, j, up, :])
+                    gain = -0.5 * fields[THICK, j, at, :]
+                    fields[WX, j, at, :] = fields[WX, j, at, :] + gain * slope_x[j]
+                    fields[WY, j, at, :] = fields[WY, j, at, :] + gain * slope_y
 
     velocity_step()
 
@@ -485,7 +481,7 @@
         velocity_step()
 
     stress_step(False)
-    velocity_step()
+    velocity_step(1, all_strips - 1, tiles)
     for pair in list(y_copies.values()) + z_copies:
         for copy in pair:
             copy.wait_send()
@@ -544,7 +540,6 @@
             pltpu.VMEM((z_slots, 3, rows, cols), i16),
             pltpu.VMEM((z_slots, 3, 8, LANES), f32),
             pltpu.VMEM((z_slots, 3, 8, LANES), f32),
-            pltpu.VMEM((3, rows, cols), f32),
             pltpu.VMEM((2, tiles, rows, LANES), jnp.int32),
             pltpu.VMEM((3, tiles + 1, tall, LANES), f32),
             pltpu.VMEM((2, FIELDS, tiles, HALO, LANES), f32),

time: 53.8 us -> 52.2 us (0.970)
  Pallas kernels: 52.3 us -> 50.7 us
    pallas_call x1, Pallas kernels: 51.3 us -> 49.7 us  [body(): pl.pallas_call(functools.partial(kernel, (secs, rows_g, cols_g, level_wei...]
where the time goes in v3:
time: 52.2 us; the launch traced here: 51.3 us
  Pallas kernels  50.7 us (97%)
  between operations  0.64 us (1%)
    pallas_call x1, Pallas kernels, body(): pl.pallas_call(functools.partial(kernel, (secs, rows_g, cols_g, level_wei...  49.7 us

profile of v3, /device:TPU:25, one launch (start us, length us, event | category | flops | bytes accessed | tf_op | source)
XLA Modules:
  0.0 51.3 jit_solution(9154855993491797721)
XLA Ops:
  0.6 49.7 %shard_map.95 = (f32[8,4,160,128]{3,2,1,0:T(8,128)S(1)}, f32[3,4,160,128]{3,2,1,0:T(8,128)S(1)}) custom-call(f32[32]{0:T(128)} %weight_ref.1, bf16[4,3,1024,384]{3,2,1,0:T(8,128)(2,1)} %ocean_hbm.1, f32[2,128,384]{2,1,0:T(8,128)} %vel_hbm.1, f32[2,128,384]{2,1,0:T(8,128)} %wind_hbm.1, f32[128,384]{1,0:T(8,128)} %thick_hbm.1, f32[128,384]{1,0:T(8,128)} %conc_hbm.1, ...), custom_call_target="tpu_custom_call" | custom-call | tf_op jit(solution)/shard_map/pallas_call | solution.py:524
  50.3 1.0 %shard_map.96 = (f32[2,128,384]{2,1,0:T(8,128)}, f32[3,128,384]{2,1,0:T(8,128)}) custom-call(f32[8,4,160,128]{3,2,1,0:T(8,128)S(1)} %get-tuple-element.4.fields, f32[3,4,160,128]{3,2,1,0:T(8,128)S(1)} %get-tuple-element.5.stress), custom_call_target="tpu_custom_call" | custom-call | tf_op jit(solution)/shard_map/pallas_call | solution.py:572
